TPU v7x, 512 devices: a whole 4x4x16 slice. The times are simulated.
512 devices in a mesh: kv: 8 (over x, core), pool: 64 (over y, z).
Axes of the slice: x: 4, y: 4, z: 16, core: 2. Of those that a mesh axis runs over, the one named last changes fastest.
Arguments:
- hidden: bfloat16 [64, 2048], P('pool'), may hold values from -6 to 6
- norm_attn: bfloat16 [2048], replicated, may hold values from 0.099609375 to 1.8984375
- wq: bfloat16 [2048, 2048], P(None, 'kv'), may hold values from -0.125 to 0.125
- wkv: bfloat16 [2, 2048, 1024], P(None, None, 'kv'), may hold values from -0.125 to 0.125
- wo: bfloat16 [2048, 2048], P('kv'), may hold values from -0.125 to 0.125
- cache: bfloat16 [2, 1024, 128, 1024], P(None, 'pool', None, 'kv'), may hold values from -70 to 70, as said below
- slot_entry: int32 [1024], P('pool'), may hold values from -1 to 4095, as said below
- lengths: int32 [64], replicated, may hold values from 1 to 8192, as said below
- norm_mlp: bfloat16 [2048], replicated, may hold values from 0.099609375 to 1.8984375
- w_gate: bfloat16 [2048, 8192], P('pool', 'kv'), may hold values from -0.125 to 0.125
- w_up: bfloat16 [2048, 8192], P('pool', 'kv'), may hold values from -0.125 to 0.125
- w_down: bfloat16 [8192, 2048], P('kv', 'pool'), may hold values from -0.0625 to 0.0625
Outputs:
- output: bfloat16 [64, 2048], P('pool')
Inputs may be any that keep to these rules, and one draw needn't show every extreme that they name: slot_entry[s] is -1 for a free slot, else r * 64 + b: the slot holds block b of request r, that is its cached positions b * 128 to b * 128 + 127 that lie below lengths[r]. Every block of every request below ceil(lengths[r] / 128) sits in exactly one slot, anywhere in the pool; a holder's slots are its 16 entries. Its new token stands at position lengths[r]. `cache`: keys and values of the cached tokens, already rotated.
All inputs are finite; a program needn't handle non-finite values.
Results may differ from a plain program's by a relative error of at most 0.012.
The roundings to bfloat16 on the way count: a program that leaves them out, or rounds other values in their place, can miss the bound.
Values may be sent and summed in bfloat16 or wider, within the bound.
A program may use at most 64 MiB of HBM per device.

v0:
```python
import math
import jax
import jax.numpy as jnp
from jax import lax
from jax.sharding import PartitionSpec as P

QUERY_HEAD_COUNT = 16
KEY_VALUE_HEADS = 8
HEAD_SIZE = 128
NEGATIVE = -1e30
EPSILON = 1e-05
ROPE_BASE = 1000000.0


def combined_all(x, axis, combine):
    everything = jax.tree.map(lambda part: lax.all_gather(part, axis), x)
    initial = jax.tree.map(lambda part: part[0], everything)

    def step(k, so_far):
        return combine(so_far, jax.tree.map(lambda part: part[k], everything))

    return lax.fori_loop(1, lax.axis_size(axis), step, initial)


def narrow_rows(tensor):
    return lax.optimization_barrier(tensor.astype(jnp.bfloat16))


def rms_scale(inputs, gain_vec):
    widened = inputs.astype(jnp.float32)
    mean_square = jnp.mean(widened * widened, axis=-1, keepdims=True)
    return narrow_rows(widened * lax.rsqrt(mean_square + EPSILON) * gain_vec.astype(jnp.float32))


def rotate(vectors, positions):
    head_width = vectors.shape[-1]
    halfway = head_width // 2
    frequency = jnp.exp(
        jnp.arange(halfway, dtype=jnp.float32) * (-2.0 * math.log(ROPE_BASE) / head_width)
    )
    angles = positions.astype(jnp.float32)[:, None] * frequency[None, :]
    cosine = jnp.cos(angles)[:, None, :]
    sine_of = jnp.sin(angles)[:, None, :]
    leading = vectors[..., :halfway]
    trailing = vectors[..., halfway:]
    return jnp.concatenate(
        [leading * cosine - trailing * sine_of, trailing * cosine + leading * sine_of], axis=-1
    )


def combine(earlier, latter):
    highest = jnp.maximum(earlier[0], latter[0])
    scale_early = jnp.exp(earlier[0] - highest)
    scale_late = jnp.exp(latter[0] - highest)
    row_count, head_count = highest.shape
    feature = earlier[2].shape[1] // head_count
    early_out = earlier[2].reshape(row_count, head_count, feature) * scale_early[:, :, None]
    late_out = latter[2].reshape(row_count, head_count, feature) * scale_late[:, :, None]
    weight_sum = earlier[1] * scale_early + latter[1] * scale_late
    return (highest, weight_sum, (early_out + late_out).reshape(row_count, head_count * feature))


def per_device(
    hidden, norm_attn, wq, wkv, wo, cache, slot_entry, lengths, norm_mlp, w_gate, w_up, w_down
):
    home_rows = hidden.shape[0]
    shared_heads = wkv.shape[2] // HEAD_SIZE
    queries_per_shared = QUERY_HEAD_COUNT // KEY_VALUE_HEADS
    query_heads = shared_heads * queries_per_shared
    home_index = lax.axis_index("pool")
    max_blocks = slot_entry.shape[0] * lax.axis_size("pool") // 16
    positions = lax.dynamic_slice_in_dim(lengths, home_index * home_rows, home_rows)
    normed_input = rms_scale(hidden, norm_attn)
    query_rows = jnp.dot(normed_input, wq, preferred_element_type=jnp.float32).reshape(
        home_rows, query_heads, HEAD_SIZE
    )
    query_rows = narrow_rows(rotate(query_rows, positions) * HEAD_SIZE ** (-0.5))
    fresh_keys = jnp.dot(normed_input, wkv[0], preferred_element_type=jnp.float32).reshape(
        home_rows, shared_heads, HEAD_SIZE
    )
    fresh_keys = narrow_rows(rotate(fresh_keys, positions))
    fresh_values = narrow_rows(
        jnp.dot(normed_input, wkv[1], preferred_element_type=jnp.float32)
    ).reshape(home_rows, shared_heads, HEAD_SIZE)
    every_query = lax.all_gather(
        query_rows.reshape(home_rows, query_heads * HEAD_SIZE), "pool", axis=0, tiled=True
    )
    request_list = every_query.shape[0]
    every_query = every_query.reshape(request_list, shared_heads, queries_per_shared, HEAD_SIZE)
    slot_count = slot_entry.shape[0]
    block_len = cache.shape[2]
    live_slot = slot_entry >= 0
    owners = jnp.where(live_slot, slot_entry // max_blocks, 0)
    block_index = jnp.where(live_slot, slot_entry % max_blocks, 0)
    picked = every_query[owners]
    block_keys = cache[0].reshape(slot_count, block_len, shared_heads, HEAD_SIZE)
    block_values = cache[1].reshape(slot_count, block_len, shared_heads, HEAD_SIZE)
    scores = jnp.einsum("sgjd,stgd->sgjt", picked, block_keys, preferred_element_type=jnp.float32)
    position = block_index[:, None] * block_len + jnp.arange(block_len, dtype=jnp.int32)[None, :]
    in_range = live_slot[:, None] & (position < lengths[owners][:, None])
    scores = jnp.where(in_range[:, None, None, :], scores, NEGATIVE)
    block_max = jnp.max(scores, axis=-1)
    same_owner = (owners[:, None] == owners[None, :]) & live_slot[:, None] & live_slot[None, :]
    holder_max = jnp.max(jnp.where(same_owner[:, :, None, None], block_max[None], NEGATIVE), axis=1)
    raised = jnp.where(in_range[:, None, None, :], jnp.exp(scores - holder_max[..., None]), 0.0)
    holder_total = jnp.sum(raised, axis=-1)
    holder_output = jnp.einsum(
        "sgjt,stgd->sgjd", narrow_rows(raised), block_values, preferred_element_type=jnp.float32
    )
    member = (owners[:, None] == jnp.arange(request_list, dtype=jnp.int32)[None, :]) & live_slot[
        :, None
    ]
    request_max = jnp.max(jnp.where(member.T[:, :, None, None], holder_max[None], NEGATIVE), axis=1)
    request_max = request_max.reshape(request_list, query_heads)
    member_float = member.astype(jnp.float32)
    request_total = jnp.einsum(
        "sr,sgj->rgj", member_float, holder_total, precision=lax.Precision.HIGHEST
    )
    request_total = request_total.reshape(request_list, query_heads)
    request_out = jnp.einsum(
        "sr,sgjd->rgjd", member_float, holder_output, precision=lax.Precision.HIGHEST
    )
    request_out = request_out.reshape(request_list, query_heads * HEAD_SIZE)
    merged = combined_all((request_max, request_total, request_out), "pool", combine)
    part_max = lax.dynamic_slice_in_dim(merged[0], home_index * home_rows, home_rows)
    part_total = lax.dynamic_slice_in_dim(merged[1], home_index * home_rows, home_rows)
    part_out = lax.dynamic_slice_in_dim(merged[2], home_index * home_rows, home_rows)
    own_query = query_rows.reshape(home_rows, shared_heads, queries_per_shared, HEAD_SIZE).astype(
        jnp.float32
    )
    new_score = jnp.sum(own_query * fresh_keys.astype(jnp.float32)[:, :, None, :], axis=-1).reshape(
        home_rows, query_heads
    )
    highest = jnp.maximum(part_max, new_score)
    old_scale = jnp.exp(part_max - highest)
    new_scale = jnp.exp(new_score - highest)
    weight_sum = part_total * old_scale + new_scale
    new_term = (
        new_scale.reshape(home_rows, shared_heads, queries_per_shared)[..., None]
        * fresh_values.astype(jnp.float32)[:, :, None, :]
    )
    combined = part_out.reshape(home_rows, query_heads, HEAD_SIZE) * old_scale[
        ..., None
    ] + new_term.reshape(home_rows, query_heads, HEAD_SIZE)
    attended = narrow_rows(combined / weight_sum[..., None]).reshape(
        home_rows, query_heads * HEAD_SIZE
    )
    projected = lax.psum(jnp.dot(attended, wo, preferred_element_type=jnp.float32), "kv")
    residual = narrow_rows(hidden.astype(jnp.float32) + projected)
    mlp_in = rms_scale(residual, norm_mlp)
    columns = lax.all_to_all(mlp_in, "pool", split_axis=1, concat_axis=0, tiled=True)
    hidden_width = w_gate.shape[1]
    gate_term = jnp.dot(columns, w_gate, preferred_element_type=jnp.float32)
    up_term = jnp.dot(columns, w_up, preferred_element_type=jnp.float32)
    summed = lax.psum_scatter(
        jnp.concatenate([gate_term, up_term], axis=1), "pool", scatter_dimension=0, tiled=True
    )
    activation = narrow_rows(jax.nn.silu(summed[:, :hidden_width]) * summed[:, hidden_width:])
    projected_down = jnp.dot(
        lax.all_gather(activation, "pool", axis=0, tiled=True),
        w_down,
        preferred_element_type=jnp.float32,
    )
    mlp_out = narrow_rows(lax.psum(projected_down, "kv"))
    returned = lax.all_to_all(mlp_out, "pool", split_axis=0, concat_axis=1, tiled=True)
    return (residual.astype(jnp.float32) + returned.astype(jnp.float32)).astype(jnp.bfloat16)


def solution(mesh):
    return jax.shard_map(
        per_device,
        mesh=mesh,
        in_specs=(
            P("pool", None),
            P(),
            P(None, "kv"),
            P(None, None, "kv"),
            P("kv", None),
            P(None, "pool", None, "kv"),
            P("pool"),
            P(),
            P(),
            P("pool", "kv"),
            P("pool", "kv"),
            P("kv", "pool"),
        ),
        out_specs=P("pool", None),
        check_vma=False,
    )
```

profile of v0, /device:TPU:8, one launch (start us, length us, event | category | flops | bytes accessed | tf_op | source)
XLA Modules:
  0.0 794.5 jit_solution(5610471597167837660)
XLA Ops:
  8.0 1.2 dynamic_slice.42
  10.6 1.3 multiply_reduce_fusion.1
  13.3 1.5 fusion.5
  15.0 88.2 %all-gather.3 = bf16[64,1,256]{2,1,0:T(2,128)(2,1)S(1)} all-gather(bf16[1,1,256]{2,1,0:T(2,128)(2,1)S(1)} %reshape.618), channel_id=1, replica_groups=mesh['kv'=8,'pool'=64] {'pool'}, dimensions={0}, use_global_device_ids=true | all-gather | bytes 33280 | tf_op jit(solution)/shard_map/all_gather | solution.py:85
  103.4 1.3 gather_fusion
  105.5 1.5 fusion.61
  107.5 1.3 fusion.10
  108.8 0.9 fusion.20
  109.8 1.2 convolution_bitcast_fusion.2
  111.2 1.2 fusion.4
  112.6 79.4 %all-gather.5 = f32[64,64,2]{1,2,0:T(2,128)S(1)} all-gather(f32[1,64,2]{1,2,0:T(2,128)S(1)} %convolution_bitcast_fusion), channel_id=3, replica_groups=mesh['kv'=8,'pool'=64] {'pool'}, dimensions={0}, use_global_device_ids=true | all-gather | bytes 33280 | tf_op jit(solution)/shard_map/all_gather | solution.py:16
  192.2 81.0 %all-gather.4 = f32[64,64,2]{1,2,0:T(2,128)S(1)} all-gather(f32[1,64,2]{1,2,0:T(2,128)S(1)} %bitcast.156), channel_id=2, replica_groups=mesh['kv'=8,'pool'=64] {'pool'}, dimensions={0}, use_global_device_ids=true | all-gather | bytes 33280 | tf_op jit(solution)/shard_map/all_gather | solution.py:16
  274.2 87.2 %while.19 = (s32[]{:T(128)}, f32[64,2]{0,1:T(2,128)S(1)}, f32[64,2]{0,1:T(2,128)S(1)}, f32[64,256]{1,0:T(8,128)S(1)}, f32[64,64,2]{1,2,0:T(2,128)S(1)}, /*index=...) while((s32[]{:T(128)}, f32[64,2]{0,1:T(2,128)S(1)}, ...), condition=%wide.region_6.7_spmd, body=%wide.region_5.6_spmd.sunk | while | flops 49925 | bytes 466071 | solution.py:22
  274.7 0.9 fusion.74
  280.2 0.9 fusion.74
  281.6 0.9 fusion.74
  362.0 12.6 %psum.14 = f32[1,2048]{1,0:T(1,128)S(1)} all-reduce(f32[1,2048]{1,0:T(1,128)S(1)} %fusion.62), channel_id=1, replica_groups=mesh['kv'=8,'pool'=64] {'kv'}, use_global_device_ids=true, to_apply=%region_8.9 | all-reduce | flops 2048 | bytes 16384 | tf_op jit(solution)/shard_map/psum | solution.py:148
  376.2 23.6 %all_to_all.30 = bf16[1,64,32]{2,0,1:T(2,128)(2,1)S(1)} all-to-all(bf16[1,64,32]{2,0,1:T(2,128)(2,1)S(1)} %all_to_all.27), channel_id=1, replica_groups=mesh['kv'=8,'pool'=64] {'pool'}, dimensions={1} | all-to-all | bytes 8192 | tf_op jit(solution)/shard_map/all_to_all | solution.py:151
  401.1 1.3 dynamic-slice
  402.4 255.3 %all-reduce.3.cloned.1.call-done = f32[64,2048]{1,0:T(8,128)} async-done(((f32[64,2048]{1,0:T(8,128)}), f32[64,2048]{1,0:T(8,128)}) %all-reduce.3.cloned.1.call-update) | async-done | bytes 524304
  657.7 1.5 fusion.39
  659.2 80.6 %all-gather.6 = bf16[64,1,1024]{2,1,0:T(2,128)(2,1)S(1)} all-gather(bf16[1,1,1024]{2,1,0:T(2,128)(2,1)S(1)} %bitcast.153), channel_id=1, replica_groups=mesh['kv'=8,'pool'=64] {'pool'}, dimensions={0}, use_global_device_ids=true | all-gather | bytes 133120 | tf_op jit(solution)/shard_map/all_gather | solution.py:160
  739.9 23.6 %psum.15 = bf16[64,32]{0,1:T(8,128)(2,1)S(1)} all-reduce(f32[64,32]{0,1:T(8,128)S(1)} %fusion.17), channel_id=1, replica_groups=mesh['kv'=8,'pool'=64] {'kv'}, use_global_device_ids=true, to_apply=%region_11.12 | all-reduce | flops 2048 | bytes 12288 | tf_op jit(solution)/shard_map/psum | solution.py:164
  763.5 23.4 %all_to_all.31 = bf16[64,1,32]{2,1,0:T(2,128)(2,1)S(1)} all-to-all(bf16[64,1,32]{2,1,0:T(2,128)(2,1)S(1)} %copy.51), channel_id=1, replica_groups=mesh['kv'=8,'pool'=64] {'pool'}, dimensions={0} | all-to-all | bytes 8192 | tf_op jit(solution)/shard_map/all_to_all | solution.py:165
  (443 shorter events, 92.0 us)
Async XLA Ops:
  6.5 355.2 %copy-start = (bf16[256,2048]{1,0:T(8,128)(2,1)S(1)}, bf16[256,2048]{1,0:T(8,128)(2,1)}, u32[]{:S(2)}) copy-start(bf16[256,2048]{1,0:T(8,128)(2,1)} %param.18) | copy-start | bytes 3145732
  6.5 105.9 %copy-start.4 = (bf16[2048]{0:T(1024)(128)(2,1)S(1)}, bf16[2048]{0:T(1024)(128)(2,1)}, u32[]{:S(2)}) copy-start(bf16[2048]{0:T(1024)(128)(2,1)} %param.22) | copy-start | bytes 12292
  6.5 266.8 %all-gather.9.cloned.1.call-start = ((), (), s32[]{:S(2)}) async-start(), calls=%async_computation.2 | async-start | bytes 4259840 | tf_op jit(solution)/shard_map/all_gather | solution.py:16
  14.8 359.9 %copy-start.1 = (bf16[1,2048]{1,0:T(2,128)(2,1)S(1)}, bf16[1,2048]{1,0:T(2,128)(2,1)}, u32[]{:S(2)}) copy-start(bf16[1,2048]{1,0:T(2,128)(2,1)} %param.14) | copy-start | bytes 12292
  15.0 384.8 %copy-start.2 = (bf16[32,1024]{1,0:T(8,128)(2,1)S(1)}, bf16[32,1024]{1,0:T(8,128)(2,1)}, u32[]{:S(2)}) copy-start(bf16[32,1024]{1,0:T(8,128)(2,1)} %param.24) | copy-start | bytes 196612
  103.4 296.6 %copy-start.3 = (bf16[32,1024]{1,0:T(8,128)(2,1)S(1)}, bf16[32,1024]{1,0:T(8,128)(2,1)}, u32[]{:S(2)}) copy-start(bf16[32,1024]{1,0:T(8,128)(2,1)} %param.23) | copy-start | bytes 196612
  109.7 547.9 %all-reduce.3.cloned.1.call-start = ((), (), s32[]{:S(2)}) async-start(), calls=%async_computation.3 | async-start | bytes 1048576
  111.0 628.7 %copy-start.5 = (bf16[1024,32]{0,1:T(8,128)(2,1)S(1)}, bf16[1024,32]{0,1:T(8,128)(2,1)}, u32[]{:S(2)}) copy-start(bf16[1024,32]{0,1:T(8,128)(2,1)} %param.25) | copy-start | bytes 196612
Sparse Core Ops, SparseCore 0:
  109.9 140.5 all-gather.8
  401.2 256.3 all-reduce.2
where the time goes:
time: 798 us; the launch traced here: 795 us
  blocking collectives  412 us (52%)
  waiting for transfers between devices  255 us (32%)
  other arithmetic  66.5 us (8%)
  local copies, waits for them, and re-layouts  33.7 us (4%)
  between operations  15.6 us (2%)
  matrix products  8.65 us (1%)
    unnamed x3, waiting for transfers between devices  255 us
    all_gather x2, blocking collectives, combined_all(): everything = jax.tree.map(lambda part: lax.all_gather(part, axis), x)  160 us
    all_gather x1, blocking collectives, per_device(): lax.all_gather(query_rows.reshape(home_rows, query_heads * HEAD_SIZE), 'p...  88.2 us
    all_gather x1, blocking collectives, per_device(): lax.all_gather(activation, 'pool', axis=0, tiled=True)  80.6 us
    add x63, other arithmetic, combine(): early_out + late_out  55.6 us
    psum x1, blocking collectives, per_device(): mlp_out = narrow_rows(lax.psum(projected_down, 'kv'))  23.6 us
    all_to_all x1, blocking collectives, per_device(): lax.all_to_all(mlp_in, 'pool', split_axis=1, concat_axis=0, tiled=True)  23.6 us
    all_to_all x1, blocking collectives, per_device(): lax.all_to_all(mlp_out, 'pool', split_axis=0, concat_axis=1, tiled=True)  23.4 us
  transfers between devices with their start and end apart: 2, of which 1 were waited for; matrix products, arithmetic and copies ran while one was open for 1% of the time, Pallas kernels for 0%

commit v1 on v0

--- a/solution.py
+++ b/solution.py
@@ -10,6 +10,11 @@
 NEGATIVE = -1e30
 EPSILON = 1e-05
 ROPE_BASE = 1000000.0
+
+
+def exchange_gather(value, mesh_axis, dim):
+    stack = jnp.stack([value] * lax.axis_size(mesh_axis))
+    return jnp.concatenate(lax.all_to_all(stack, mesh_axis, 0, 0), axis=dim)
 
 
 def combined_all(x, axis, combine):
@@ -157,9 +162,7 @@
     )
     activation = narrow_rows(jax.nn.silu(summed[:, :hidden_width]) * summed[:, hidden_width:])
     projected_down = jnp.dot(
-        lax.all_gather(activation, "pool", axis=0, tiled=True),
-        w_down,
-        preferred_element_type=jnp.float32,
+        exchange_gather(activation, "pool", 0), w_down, preferred_element_type=jnp.float32
     )
     mlp_out = narrow_rows(lax.psum(projected_down, "kv"))
     returned = lax.all_to_all(mlp_out, "pool", split_axis=0, concat_axis=1, tiled=True)

time: 798 us -> 740 us (0.927)
  blocking collectives: 412 us -> 352 us
    all_gather x1 -> x0, blocking collectives: 80.6 us -> none  [per_device(): lax.all_gather(activation, 'pool', axis=0, tiled=True)]
    all_to_all x0 -> x1, blocking collectives: none -> 23.9 us  [exchange_gather(): return jnp.concatenate(lax.all_to_all(stack, mesh_axis, 0, 0), axis=dim)]
where the time goes in v1:
time: 740 us; the launch traced here: 737 us
  blocking collectives  352 us (48%)
  waiting for transfers between devices  255 us (34%)
  other arithmetic  67.9 us (9%)
  local copies, waits for them, and re-layouts  34.6 us (5%)
  between operations  15.6 us (2%)
  matrix products  8.64 us (1%)
    unnamed x3, waiting for transfers between devices  255 us
    all_gather x2, blocking collectives, combined_all(): everything = jax.tree.map(lambda part: lax.all_gather(part, axis), x)  160 us
    all_gather x1, blocking collectives, per_device(): lax.all_gather(query_rows.reshape(home_rows, query_heads * HEAD_SIZE), 'p...  88.2 us
    add x63, other arithmetic, combine(): early_out + late_out  55.6 us
    all_to_all x1, blocking collectives, exchange_gather(): return jnp.concatenate(lax.all_to_all(stack, mesh_axis, 0, 0), axis=dim)  23.9 us
    psum x1, blocking collectives, per_device(): mlp_out = narrow_rows(lax.psum(projected_down, 'kv'))  23.6 us
    all_to_all x1, blocking collectives, per_device(): lax.all_to_all(mlp_in, 'pool', split_axis=1, concat_axis=0, tiled=True)  23.6 us
    all_to_all x1, blocking collectives, per_device(): lax.all_to_all(mlp_out, 'pool', split_axis=0, concat_axis=1, tiled=True)  19.8 us
  transfers between devices with their start and end apart: 2, of which 1 were waited for; matrix products, arithmetic and copies ran while one was open for 1% of the time, Pallas kernels for 0%

profile of v1, /device:TPU:8, one launch (start us, length us, event | category | flops | bytes accessed | tf_op | source)
XLA Modules:
  0.0 736.6 jit_solution(7008568991899991825)
XLA Ops:
  8.0 1.2 dynamic_slice.42
  10.6 1.3 multiply_reduce_fusion.1
  13.3 1.5 fusion.5
  15.0 88.2 %all-gather.3 = bf16[64,1,256]{2,1,0:T(2,128)(2,1)S(1)} all-gather(bf16[1,1,256]{2,1,0:T(2,128)(2,1)S(1)} %reshape.625), channel_id=1, replica_groups=mesh['kv'=8,'pool'=64] {'pool'}, dimensions={0}, use_global_device_ids=true | all-gather | bytes 33280 | tf_op jit(solution)/shard_map/all_gather | solution.py:90
  103.4 1.3 gather_fusion
  105.5 1.5 fusion.61
  107.5 1.3 fusion.10
  108.8 0.9 fusion.20
  109.8 1.2 convolution_bitcast_fusion.2
  111.2 1.2 fusion.4
  112.6 79.4 %all-gather.5 = f32[64,64,2]{1,2,0:T(2,128)S(1)} all-gather(f32[1,64,2]{1,2,0:T(2,128)S(1)} %convolution_bitcast_fusion), channel_id=3, replica_groups=mesh['kv'=8,'pool'=64] {'pool'}, dimensions={0}, use_global_device_ids=true | all-gather | bytes 33280 | tf_op jit(solution)/shard_map/all_gather | solution.py:21
  192.2 81.0 %all-gather.4 = f32[64,64,2]{1,2,0:T(2,128)S(1)} all-gather(f32[1,64,2]{1,2,0:T(2,128)S(1)} %bitcast.154), channel_id=2, replica_groups=mesh['kv'=8,'pool'=64] {'pool'}, dimensions={0}, use_global_device_ids=true | all-gather | bytes 33280 | tf_op jit(solution)/shard_map/all_gather | solution.py:21
  274.2 87.2 %while.19 = (s32[]{:T(128)}, f32[64,2]{0,1:T(2,128)S(1)}, f32[64,2]{0,1:T(2,128)S(1)}, f32[64,256]{1,0:T(8,128)S(1)}, f32[64,64,2]{1,2,0:T(2,128)S(1)}, /*index=...) while((s32[]{:T(128)}, f32[64,2]{0,1:T(2,128)S(1)}, ...), condition=%wide.region_6.7_spmd, body=%wide.region_5.6_spmd.sunk | while | flops 49925 | bytes 466071 | solution.py:27
  277.5 0.9 fusion.74
  278.8 0.9 fusion.74
  362.0 12.6 %psum.14 = f32[1,2048]{1,0:T(1,128)S(1)} all-reduce(f32[1,2048]{1,0:T(1,128)S(1)} %fusion.62), channel_id=1, replica_groups=mesh['kv'=8,'pool'=64] {'kv'}, use_global_device_ids=true, to_apply=%region_8.9 | all-reduce | flops 2048 | bytes 16384 | tf_op jit(solution)/shard_map/psum | solution.py:153
  376.2 23.6 %all_to_all.35 = bf16[1,64,32]{2,0,1:T(2,128)(2,1)S(1)} all-to-all(bf16[1,64,32]{2,0,1:T(2,128)(2,1)S(1)} %all_to_all.31), channel_id=1, replica_groups=mesh['kv'=8,'pool'=64] {'pool'}, dimensions={1} | all-to-all | bytes 8192 | tf_op jit(solution)/shard_map/all_to_all | solution.py:156
  401.1 1.3 dynamic-slice
  402.4 255.3 %all-reduce.3.cloned.1.call-done = f32[64,2048]{1,0:T(8,128)} async-done(((f32[64,2048]{1,0:T(8,128)}), f32[64,2048]{1,0:T(8,128)}) %all-reduce.3.cloned.1.call-update) | async-done | bytes 524304
  657.7 1.5 fusion.39
  659.9 1.4 reduce.17
  661.3 23.9 %all_to_all.36 = bf16[64,2,512]{2,1,0:T(2,128)(2,1)S(1)} all-to-all(bf16[64,2,512]{2,1,0:T(2,128)(2,1)S(1)} %reshape.659), channel_id=1, replica_groups=mesh['kv'=8,'pool'=64] {'pool'}, dimensions={0} | all-to-all | bytes 262144 | tf_op jit(solution)/shard_map/all_to_all | solution.py:17
  685.5 23.6 %psum.15 = bf16[64,32]{0,1:T(8,128)(2,1)S(1)} all-reduce(f32[64,32]{0,1:T(8,128)S(1)} %fusion.17), channel_id=1, replica_groups=mesh['kv'=8,'pool'=64] {'kv'}, use_global_device_ids=true, to_apply=%region_11.12 | all-reduce | flops 2048 | bytes 12288 | tf_op jit(solution)/shard_map/psum | solution.py:167
  709.2 19.8 %all_to_all.37 = bf16[64,1,32]{2,1,0:T(2,128)(2,1)S(1)} all-to-all(bf16[64,1,32]{2,1,0:T(2,128)(2,1)S(1)} %copy.51), channel_id=1, replica_groups=mesh['kv'=8,'pool'=64] {'pool'}, dimensions={0} | all-to-all | bytes 8192 | tf_op jit(solution)/shard_map/all_to_all | solution.py:168
  (449 shorter events, 93.7 us)
Async XLA Ops:
  6.5 355.2 %copy-start = (bf16[256,2048]{1,0:T(8,128)(2,1)S(1)}, bf16[256,2048]{1,0:T(8,128)(2,1)}, u32[]{:S(2)}) copy-start(bf16[256,2048]{1,0:T(8,128)(2,1)} %param.18) | copy-start | bytes 3145732
  6.5 105.9 %copy-start.4 = (bf16[2048]{0:T(1024)(128)(2,1)S(1)}, bf16[2048]{0:T(1024)(128)(2,1)}, u32[]{:S(2)}) copy-start(bf16[2048]{0:T(1024)(128)(2,1)} %param.22) | copy-start | bytes 12292
  6.5 266.8 %all-gather.8.cloned.1.call-start = ((), (), s32[]{:S(2)}) async-start(), calls=%async_computation.3 | async-start | bytes 4259840 | tf_op jit(solution)/shard_map/all_gather | solution.py:21
  14.8 359.9 %copy-start.1 = (bf16[1,2048]{1,0:T(2,128)(2,1)S(1)}, bf16[1,2048]{1,0:T(2,128)(2,1)}, u32[]{:S(2)}) copy-start(bf16[1,2048]{1,0:T(2,128)(2,1)} %param.14) | copy-start | bytes 12292
  15.0 384.8 %copy-start.2 = (bf16[32,1024]{1,0:T(8,128)(2,1)S(1)}, bf16[32,1024]{1,0:T(8,128)(2,1)}, u32[]{:S(2)}) copy-start(bf16[32,1024]{1,0:T(8,128)(2,1)} %param.24) | copy-start | bytes 196612
  103.4 296.6 %copy-start.3 = (bf16[32,1024]{1,0:T(8,128)(2,1)S(1)}, bf16[32,1024]{1,0:T(8,128)(2,1)}, u32[]{:S(2)}) copy-start(bf16[32,1024]{1,0:T(8,128)(2,1)} %param.23) | copy-start | bytes 196612
  109.7 547.9 %all-reduce.3.cloned.1.call-start = ((), (), s32[]{:S(2)}) async-start(), calls=%async_computation.4 | async-start | bytes 1048576
  274.2 411.1 %copy-start.5 = (bf16[1024,32]{0,1:T(8,128)(2,1)S(1)}, bf16[1024,32]{0,1:T(8,128)(2,1)}, u32[]{:S(2)}) copy-start(bf16[1024,32]{0,1:T(8,128)(2,1)} %param.25) | copy-start | bytes 196612
Sparse Core Ops, SparseCore 0:
  109.9 140.5 all-gather.7
  401.2 256.3 all-reduce.2
